TPU v7x, 32 devices: a whole 2x2x4 slice. The times are simulated.
32 devices in a mesh: shard: 4 (over z), ctx: 2 (over core), tp: 4 (over y, x).
Axes of the slice: x: 2, y: 2, z: 4, core: 2. Of those that a mesh axis runs over, the one named last changes fastest.
Arguments:
- tokens: bfloat16 [8, 2048, 768], P('shard', 'ctx'), may hold values from -6 to 6
- segment_ids: int32 [8, 2048], P('shard', 'ctx'), may hold values from 0 to 34, as said below
- offsets: int32 [8, 2048], P('shard', 'ctx'), may hold values from 0 to 799, as said below
- qkv_weight: bfloat16 [768, 3, 768], P(('shard', 'ctx'), None, 'tp'), may hold values from -0.3125 to 0.3125
- out_weight: bfloat16 [768, 768], P(('shard', 'ctx'), 'tp'), may hold values from -0.875 to 0.875
- ffn_weight: bfloat16 [768, 2, 3072], P(('shard', 'ctx'), None, 'tp'), may hold values from -0.21875 to 0.21875
- qkv_bias: float32 [3, 768], P(None, 'tp'), may hold values from -3 to 3
- ffn_bias: float32 [3072], P('tp'), may hold values from -3 to 3
- norm_gain: float32 [2, 768], replicated, may hold values from 0.5 to 1.5
- shift_params: float32 [4, 768], replicated, may hold values from -3 to 3
- out_grad: bfloat16 [8, 2048, 768], P('shard', 'ctx'), may hold values from -6 to 6
Outputs:
- outputs: bfloat16 [8, 2048, 768], P('shard', 'ctx')
- grad_tokens: bfloat16 [8, 2048, 768], P('shard', 'ctx')
- grad_qkv_weight: float32 [768, 3, 768], P(('shard', 'ctx'), None, 'tp')
- grad_out_weight: float32 [768, 768], P(('shard', 'ctx'), 'tp')
- grad_ffn_weight: float32 [768, 2, 3072], P(('shard', 'ctx'), None, 'tp')
- grad_qkv_bias: float32 [3, 768], P(None, 'tp')
- grad_ffn_bias: float32 [3072], P('tp')
- grad_norm_gain: float32 [2, 768], replicated
- grad_shift_params: float32 [4, 768], replicated
Inputs may be any that keep to these rules, and one draw needn't show every extreme that they name: `segment_ids`: segment numbers start at 0 in each sequence and rise by one where a new document begins. offsets are 0 at a document's first token and rise by one along it; a document has at most 800 tokens, and every document but a sequence's last has at least 60.
All inputs are finite; a program needn't handle non-finite values.
Results may differ from a plain program's by a relative error of at most 0.017.
The roundings to bfloat16 on the way count: a program that leaves them out, or rounds other values in their place, can miss the bound.
Values may be sent and summed in bfloat16 or wider, within the bound.
No kernel may reach another device: no remote copies, remote signals or barrier semaphores. Data moves between devices by JAX's collectives and lax.ppermute only.
A program may use at most 192 MiB of HBM per device.

v0:
```python
from functools import partial
import jax
import jax.numpy as jnp
from jax import lax
from jax.sharding import PartitionSpec as P

HEAD = 64
EPSILON = 1e-12


def rotate_pairs(values, offsets, direction):
    half_size = values.shape[-1] // 2
    frequency = 10000.0 ** (-2.0 * jnp.arange(half_size, dtype=jnp.float32) / values.shape[-1])
    angles = offsets.astype(jnp.float32)[:, None] * frequency[None, :]
    cosine = jnp.cos(angles)[:, None, :]
    sine_part = direction * jnp.sin(angles)[:, None, :]
    paired = values.reshape(values.shape[:-1] + (half_size, 2))
    even_part = paired[..., 0]
    odd_part = paired[..., 1]
    turned = jnp.stack(
        [even_part * cosine - odd_part * sine_part, even_part * sine_part + odd_part * cosine],
        axis=-1,
    )
    return turned.reshape(values.shape)


def norm_parts(rows_in):
    centre = rows_in - jnp.mean(rows_in, axis=-1, keepdims=True)
    inverse_root = lax.rsqrt(jnp.mean(centre * centre, axis=-1, keepdims=True) + EPSILON)
    return (centre * inverse_root, inverse_root)


def norm_back(grad_in, scaled, inverse_root, gain_row):
    grad_scaled = grad_in * gain_row
    term_mean = jnp.mean(grad_scaled, axis=-1, keepdims=True)
    term_along = jnp.mean(grad_scaled * scaled, axis=-1, keepdims=True)
    return inverse_root * (grad_scaled - term_mean - scaled * term_along)


def attention_weights(qkv_weight, out_weight):
    return (
        lax.all_gather(qkv_weight, ("shard", "ctx"), axis=0, tiled=True),
        lax.all_gather(out_weight, ("shard", "ctx"), axis=0, tiled=True),
    )


def feed_weights(ffn_weight):
    return lax.all_gather(ffn_weight, ("shard", "ctx"), axis=0, tiled=True)


def masked_scores(queries, keys_all, same_doc, score_scale):
    scores = (
        jnp.einsum("shd,thd->hst", queries, keys_all, preferred_element_type=jnp.float32)
        * score_scale
    )
    return jnp.where(same_doc, scores, -1e30)


def contract_last(left, right):
    return lax.dot_general(
        left, right, (((1,), (1,)), ((), ())), preferred_element_type=jnp.float32
    )


def contract_first(left, right):
    return lax.dot_general(
        left, right, (((0,), (0,)), ((), ())), preferred_element_type=jnp.float32
    )


def body(
    tokens,
    segment_ids,
    offsets,
    qkv_weight,
    out_weight,
    ffn_weight,
    qkv_bias,
    ffn_bias,
    norm_gain,
    shift_params,
    out_grad,
):
    model_width = tokens.shape[2]
    part_width = qkv_weight.shape[2]
    hidden_width = ffn_weight.shape[2]
    local_heads = part_width // HEAD
    score_scale = HEAD ** (-0.5)
    tp_count = lax.axis_size("tp")
    tp_rank = lax.axis_index("tp")

    def micro_step(totals, micro_batch):
        tokens_mb, segment_mb, offsets_mb, grad_mb = micro_batch
        half_len = tokens_mb.shape[0]
        share_len = half_len // tp_count
        share_start = tp_rank * share_len

        def share_rows(rows):
            return lax.dynamic_slice_in_dim(rows, share_start, share_len, 0)

        qkv_full, out_full = attention_weights(qkv_weight, out_weight)
        ffn_full = feed_weights(ffn_weight)
        projected = (
            jnp.einsum("sd,dke->kse", tokens_mb, qkv_full, preferred_element_type=jnp.float32)
            + qkv_bias[:, None, :]
        )
        per_head = projected.reshape(3, half_len, local_heads, HEAD)
        queries = rotate_pairs(per_head[0], offsets_mb, 1.0).astype(jnp.bfloat16)
        keys_own = rotate_pairs(per_head[1], offsets_mb, 1.0).astype(jnp.bfloat16)
        values_own = per_head[2].astype(jnp.bfloat16)
        pair_own = jnp.stack([keys_own, values_own]).reshape(2, half_len, part_width)
        segment_own = segment_mb.astype(jnp.bfloat16)
        pair_all, segment_all = (
            lax.all_gather(pair_own, "ctx", axis=1, tiled=True),
            lax.all_gather(segment_own, "ctx", axis=0, tiled=True),
        )
        seq_len = pair_all.shape[1]
        keys_all = pair_all[0].reshape(seq_len, local_heads, HEAD)
        values_all = pair_all[1].reshape(seq_len, local_heads, HEAD)
        same_doc = (segment_own[:, None] == segment_all[None, :])[None]
        scores = masked_scores(queries, keys_all, same_doc, score_scale)
        row_top = jnp.max(scores, axis=-1, keepdims=True)
        exponent = jnp.exp(scores - row_top)
        row_total = jnp.sum(exponent, axis=-1, keepdims=True)
        probs_b = (exponent / row_total).astype(jnp.bfloat16)
        log_total = row_top + jnp.log(row_total)
        context = jnp.einsum(
            "hst,thd->shd", probs_b, values_all, preferred_element_type=jnp.float32
        )
        context = context.reshape(half_len, part_width).astype(jnp.bfloat16)
        attended = lax.psum(contract_last(context, out_full), "tp")
        first_scaled, first_root = norm_parts(
            tokens_mb.astype(jnp.float32) + attended + shift_params[2]
        )
        normed = first_scaled * norm_gain[0] + shift_params[0]
        normed_b = normed.astype(jnp.bfloat16)
        hidden_in = (
            jnp.dot(normed_b, ffn_full[:, 0, :], preferred_element_type=jnp.float32) + ffn_bias
        )
        activated, gelu_pull = jax.vjp(partial(jax.nn.gelu, approximate=False), hidden_in)
        activated_b = activated.astype(jnp.bfloat16)
        returned = lax.psum(contract_last(activated_b, ffn_full[:, 1, :]), "tp")
        second_scaled, second_root = norm_parts(normed + returned + shift_params[3])
        layer_out = (second_scaled * norm_gain[1] + shift_params[1]).astype(jnp.bfloat16)
        qkv_back, out_back = attention_weights(qkv_weight, out_weight)
        ffn_back = feed_weights(ffn_weight)
        grad_top = grad_mb.astype(jnp.float32)
        grad_gain_two = jnp.sum(share_rows(grad_top) * share_rows(second_scaled), axis=0)
        grad_second = norm_back(grad_top, second_scaled, second_root, norm_gain[1])
        grad_second_b = grad_second.astype(jnp.bfloat16)
        grad_down = contract_first(grad_second_b, activated_b)
        grad_act = jnp.dot(grad_second_b, ffn_back[:, 1, :], preferred_element_type=jnp.float32)
        grad_hidden = gelu_pull(grad_act)[0].astype(jnp.bfloat16)
        grad_up = contract_first(normed_b, grad_hidden)
        grad_ffn_bias = jnp.sum(grad_hidden.astype(jnp.float32), axis=0)
        ffn_part = contract_last(grad_hidden, ffn_back[:, 0, :])
        grad_normed = grad_second + lax.psum(ffn_part, "tp")
        grad_first = norm_back(grad_normed, first_scaled, first_root, norm_gain[0])
        grad_first_b = grad_first.astype(jnp.bfloat16)
        normed_part = share_rows(grad_normed)
        first_part = share_rows(grad_first)
        grad_gain_one = jnp.sum(normed_part * share_rows(first_scaled), axis=0)
        grad_out_proj = contract_first(grad_first_b, context)
        grad_context = jnp.dot(grad_first_b, out_back, preferred_element_type=jnp.float32).astype(
            jnp.bfloat16
        )
        grad_context = grad_context.reshape(half_len, local_heads, HEAD)
        scores_again = masked_scores(queries, keys_all, same_doc, score_scale)
        probs = jnp.exp(scores_again - log_total)
        probs_again = probs.astype(jnp.bfloat16)
        grad_probs = jnp.einsum(
            "shd,thd->hst", grad_context, values_all, preferred_element_type=jnp.float32
        )
        row_dot = jnp.sum(probs * grad_probs, axis=-1, keepdims=True)
        grad_scores = (probs * (grad_probs - row_dot)).astype(jnp.bfloat16)
        grad_queries = (
            jnp.einsum("hst,thd->shd", grad_scores, keys_all, preferred_element_type=jnp.float32)
            * score_scale
        )
        grad_keys = (
            jnp.einsum("hst,shd->thd", grad_scores, queries, preferred_element_type=jnp.float32)
            * score_scale
        )
        grad_values = jnp.einsum(
            "hst,shd->thd", probs_again, grad_context, preferred_element_type=jnp.float32
        )
        grad_pair = lax.psum_scatter(
            jnp.stack([grad_keys, grad_values]).reshape(2, seq_len, part_width),
            "ctx",
            scatter_dimension=1,
            tiled=True,
        )
        grad_pair = grad_pair.reshape(2, half_len, local_heads, HEAD)
        grad_proj = jnp.stack(
            [
                rotate_pairs(grad_queries, offsets_mb, -1.0),
                rotate_pairs(grad_pair[0], offsets_mb, -1.0),
                grad_pair[1],
            ]
        )
        grad_proj = grad_proj.reshape(3, half_len, part_width).astype(jnp.bfloat16)
        grad_qkv_bias = jnp.sum(grad_proj.astype(jnp.float32), axis=1)
        grad_qkv = jnp.einsum(
            "sd,kse->dke", tokens_mb, grad_proj, preferred_element_type=jnp.float32
        )
        grad_branch = jnp.einsum(
            "kse,dke->sd", grad_proj, qkv_back, preferred_element_type=jnp.float32
        )
        grad_inputs = (grad_first + lax.psum(grad_branch, "tp")).astype(jnp.bfloat16)
        grad_shift = jnp.stack(
            [
                jnp.sum(normed_part, axis=0),
                jnp.sum(share_rows(grad_top), axis=0),
                jnp.sum(first_part, axis=0),
                jnp.sum(share_rows(grad_second), axis=0),
            ]
        )
        grad_gain = jnp.stack([grad_gain_one, grad_gain_two])
        grad_ffn = jnp.stack([grad_up, grad_down], axis=1)
        updated = (
            totals[0] + grad_qkv,
            totals[1] + grad_out_proj,
            totals[2] + grad_ffn,
            totals[3] + grad_qkv_bias,
            totals[4] + grad_ffn_bias,
            totals[5] + grad_gain,
            totals[6] + grad_shift,
        )
        return (updated, (layer_out, grad_inputs))

    zero_grads = (
        jnp.zeros((model_width, 3, part_width), jnp.float32),
        jnp.zeros((model_width, part_width), jnp.float32),
        jnp.zeros((model_width, 2, hidden_width), jnp.float32),
        jnp.zeros((3, part_width), jnp.float32),
        jnp.zeros((hidden_width,), jnp.float32),
        jnp.zeros((2, model_width), jnp.float32),
        jnp.zeros((4, model_width), jnp.float32),
    )
    totals, (outputs, grad_tokens) = lax.scan(
        micro_step, zero_grads, (tokens, segment_ids, offsets, out_grad)
    )
    grad_qkv_weight, grad_out_weight, grad_ffn_weight = (
        lax.psum_scatter(totals[0], ("shard", "ctx"), scatter_dimension=0, tiled=True),
        lax.psum_scatter(totals[1], ("shard", "ctx"), scatter_dimension=0, tiled=True),
        lax.psum_scatter(totals[2], ("shard", "ctx"), scatter_dimension=0, tiled=True),
    )
    placed_qkv = lax.dynamic_update_slice(
        jnp.zeros((3, part_width * tp_count), jnp.float32),
        totals[3],
        (jnp.int32(0), tp_rank * part_width),
    )
    placed_ffn = lax.dynamic_update_slice(
        jnp.zeros((hidden_width * tp_count,), jnp.float32), totals[4], (tp_rank * hidden_width,)
    )
    summed_qkv, summed_ffn, grad_norm_gain, grad_shift_params = lax.psum(
        (placed_qkv, placed_ffn, totals[5], totals[6]), ("shard", "ctx", "tp")
    )
    grad_qkv_bias = lax.dynamic_slice_in_dim(summed_qkv, tp_rank * part_width, part_width, 1)
    grad_ffn_bias = lax.dynamic_slice_in_dim(summed_ffn, tp_rank * hidden_width, hidden_width, 0)
    return (
        outputs,
        grad_tokens,
        grad_qkv_weight,
        grad_out_weight,
        grad_ffn_weight,
        grad_qkv_bias,
        grad_ffn_bias,
        grad_norm_gain,
        grad_shift_params,
    )


def solution(mesh):
    return jax.shard_map(
        body,
        mesh=mesh,
        in_specs=(
            P("shard", "ctx", None),
            P("shard", "ctx"),
            P("shard", "ctx"),
            P(("shard", "ctx"), None, "tp"),
            P(("shard", "ctx"), "tp"),
            P(("shard", "ctx"), None, "tp"),
            P(None, "tp"),
            P("tp"),
            P(),
            P(),
            P("shard", "ctx", None),
        ),
        out_specs=(
            P("shard", "ctx", None),
            P("shard", "ctx", None),
            P(("shard", "ctx"), None, "tp"),
            P(("shard", "ctx"), "tp"),
            P(("shard", "ctx"), None, "tp"),
            P(None, "tp"),
            P("tp"),
            P(),
            P(),
        ),
        check_vma=False,
    )
```

profile of v0, /device:TPU:0, one launch (start us, length us, event | category | flops | bytes accessed | tf_op | source)
XLA Modules:
  0.0 1406.7 jit_solution(18068525269604240569)
XLA Ops:
  10.9 1200.5 %while.29 = (s32[]{:T(128)}, f32[768,3,192]{0,2,1:T(8,128)}, f32[768,192]{0,1:T(8,128)}, f32[768,2,768]{2,0,1:T(8,128)}, f32[3,192]{1,0:T(4,128)}, /*index=5*/f3...) while((s32[]{:T(128)}, f32[768,3,192]{0,2,1:T(8,128)}, ...), condition=%wide.region_25.26_spmd.clone, body=%wide.region_0.25_spmd.clone.sunk | while | flops 15947476992 | bytes 964769600 | solution.py:240
  10.9 23.1 %all_gather.42 = bf16[768,3,192]{2,1,0:T(4,128)(2,1)} all-gather(bf16[96,3,192]{2,1,0:T(4,128)(2,1)S(1)} %get-tuple-element.828), channel_id=1, replica_groups=mesh['shard'=4,'ctx'=2,'tp'=4] {'shard','ctx'}, dimensions={0}, use_global_device_ids=true | all-gather | bytes 995328 | tf_op jit(solution)/shard_map/while/body/eval_jaxpr/all_gather | solution.py:42
  34.0 3.4 copy.39
  48.1 4.2 subtract_convert_fusion.6
  63.8 16.3 %all_gather.41 = bf16[768,192]{1,0:T(8,128)(2,1)} all-gather(bf16[96,192]{1,0:T(8,128)(2,1)} %get-tuple-element.832), channel_id=1, replica_groups=mesh['shard'=4,'ctx'=2,'tp'=4] {'shard','ctx'}, dimensions={0}, use_global_device_ids=true | all-gather | bytes 331776 | tf_op jit(solution)/shard_map/while/body/eval_jaxpr/all_gather | solution.py:43
  84.7 11.0 fusion.150
  95.6 10.4 fusion.151
  106.1 10.6 fusion.152
  122.3 84.8 %all-reduce.10.cloned.1.call-done = f32[1024,768]{1,0:T(8,128)} async-done(((f32[1024,768]{1,0:T(8,128)}), f32[1024,768]{1,0:T(8,128)}) %all-reduce.10.cloned.1.call-update) | async-done | bytes 3145744 | tf_op jit(solution)/shard_map/while/body/eval_jaxpr/psum | solution.py:131
  212.1 11.2 multiply_convert_fusion.4
  224.5 3.2 fusion.155
  228.0 87.1 %all-reduce.12.cloned.1.call-done = f32[1024,768]{1,0:T(8,128)} async-done(((f32[1024,768]{1,0:T(8,128)}), f32[1024,768]{1,0:T(8,128)}) %all-reduce.12.cloned.1.call-update) | async-done | bytes 3145744 | tf_op jit(solution)/shard_map/while/body/eval_jaxpr/psum | solution.py:142
  335.9 86.1 %all-reduce.14.cloned.1.call-done = f32[1024,768]{1,0:T(8,128)} async-done(((f32[1024,768]{1,0:T(8,128)}), f32[1024,768]{1,0:T(8,128)}) %all-reduce.14.cloned.1.call-update) | async-done | bytes 3145744 | tf_op jit(solution)/shard_map/while/body/eval_jaxpr/psum | solution.py:157
  422.0 3.6 multiply_reduce_fusion.13
  430.4 11.4 fusion.160
  441.8 16.4 %multiply_reduce_fusion.14 = (f32[3,1024]{1,0:T(4,128)}, f32[3,1024,2048]{2,1,0:T(8,128)}) fusion(f32[3,1024,2048]{2,1,0:T(8,128)} %get-tuple-element.731, f32[3,1024]{1,0:T(4,128)S(1)} %log_add_fusion.2, bf16[1024,3,64]{0,2,1:T(8,128)(2,1)} %bitcast.223, bf16[2048,3,64]{0,2,1:T(8,128)(2,1)} %bitcast.227), kind=kOutput, calls=%fused_computation.1.clone.1 | convolution fusion | flops 824177664 | bytes 51535872 | tf_op jit(solution)/shard_map/while/body/eval_jaxpr/shd,thd->hst/dot_general | solution.py:171
  458.2 16.8 %multiply_convert_fusion.5 = bf16[3,1024,2048]{2,1,0:T(8,128)(2,1)S(1)} fusion(f32[3,1024,2048]{2,1,0:T(8,128)} %get-tuple-element.750, f32[3,1024,2048]{2,1,0:T(8,128)} %get-tuple-element.731, f32[3,1024]{1,0:T(4,128)} %get-tuple-element.751, f32[3,1024]{1,0:T(4,128)S(1)} %log_add_fusion.2), kind=kLoop, calls=%fused_computation.clone.1 | loop fusion | flops 25165824 | bytes 62939136 | tf_op jit(solution)/shard_map/while/body/eval_jaxpr/convert_element_type | solution.py:175
  485.2 10.5 fusion.161
  502.9 3.8 subtract_convert_fusion.7
  521.3 4.0 convolution_bitcast_fusion.6
  536.2 70.3 %all-reduce.16.cloned.1.call-done = f32[1024,768]{1,0:T(8,128)} async-done(((f32[1024,768]{1,0:T(8,128)}), f32[1024,768]{1,0:T(8,128)}) %all-reduce.16.cloned.1.call-update) | async-done | bytes 3145744 | tf_op jit(solution)/shard_map/while/body/eval_jaxpr/psum | solution.py:209
  606.5 3.4 fusion.164
  610.1 21.4 %all_gather.42 = bf16[768,3,192]{2,1,0:T(4,128)(2,1)} all-gather(bf16[96,3,192]{2,1,0:T(4,128)(2,1)S(1)} %get-tuple-element.828), channel_id=1, replica_groups=mesh['shard'=4,'ctx'=2,'tp'=4] {'shard','ctx'}, dimensions={0}, use_global_device_ids=true | all-gather | bytes 995328 | tf_op jit(solution)/shard_map/while/body/eval_jaxpr/all_gather | solution.py:42
  631.5 3.4 copy.39
  645.6 4.2 subtract_convert_fusion.6
  661.3 16.0 %all_gather.41 = bf16[768,192]{1,0:T(8,128)(2,1)} all-gather(bf16[96,192]{1,0:T(8,128)(2,1)} %get-tuple-element.832), channel_id=1, replica_groups=mesh['shard'=4,'ctx'=2,'tp'=4] {'shard','ctx'}, dimensions={0}, use_global_device_ids=true | all-gather | bytes 331776 | tf_op jit(solution)/shard_map/while/body/eval_jaxpr/all_gather | solution.py:43
  681.8 11.0 fusion.150
  692.8 10.4 fusion.151
  703.3 10.6 fusion.152
  719.7 83.5 %all-reduce.10.cloned.1.call-done = f32[1024,768]{1,0:T(8,128)} async-done(((f32[1024,768]{1,0:T(8,128)}), f32[1024,768]{1,0:T(8,128)}) %all-reduce.10.cloned.1.call-update) | async-done | bytes 3145744 | tf_op jit(solution)/shard_map/while/body/eval_jaxpr/psum | solution.py:131
  808.3 11.2 multiply_convert_fusion.4
  824.1 87.2 %all-reduce.12.cloned.1.call-done = f32[1024,768]{1,0:T(8,128)} async-done(((f32[1024,768]{1,0:T(8,128)}), f32[1024,768]{1,0:T(8,128)}) %all-reduce.12.cloned.1.call-update) | async-done | bytes 3145744 | tf_op jit(solution)/shard_map/while/body/eval_jaxpr/psum | solution.py:142
  931.9 86.4 %all-reduce.14.cloned.1.call-done = f32[1024,768]{1,0:T(8,128)} async-done(((f32[1024,768]{1,0:T(8,128)}), f32[1024,768]{1,0:T(8,128)}) %all-reduce.14.cloned.1.call-update) | async-done | bytes 3145744 | tf_op jit(solution)/shard_map/while/body/eval_jaxpr/psum | solution.py:157
  1018.2 3.6 multiply_reduce_fusion.13
  1026.6 11.4 fusion.160
  1038.0 16.4 %multiply_reduce_fusion.14 = (f32[3,1024]{1,0:T(4,128)}, f32[3,1024,2048]{2,1,0:T(8,128)}) fusion(f32[3,1024,2048]{2,1,0:T(8,128)} %get-tuple-element.731, f32[3,1024]{1,0:T(4,128)S(1)} %log_add_fusion.2, bf16[1024,3,64]{0,2,1:T(8,128)(2,1)} %bitcast.223, bf16[2048,3,64]{0,2,1:T(8,128)(2,1)} %bitcast.227), kind=kOutput, calls=%fused_computation.1.clone.1 | convolution fusion | flops 824177664 | bytes 51535872 | tf_op jit(solution)/shard_map/while/body/eval_jaxpr/shd,thd->hst/dot_general | solution.py:171
  1054.4 16.8 %multiply_convert_fusion.5 = bf16[3,1024,2048]{2,1,0:T(8,128)(2,1)S(1)} fusion(f32[3,1024,2048]{2,1,0:T(8,128)} %get-tuple-element.750, f32[3,1024,2048]{2,1,0:T(8,128)} %get-tuple-element.731, f32[3,1024]{1,0:T(4,128)} %get-tuple-element.751, f32[3,1024]{1,0:T(4,128)S(1)} %log_add_fusion.2), kind=kLoop, calls=%fused_computation.clone.1 | loop fusion | flops 25165824 | bytes 62939136 | tf_op jit(solution)/shard_map/while/body/eval_jaxpr/convert_element_type | solution.py:175
  1081.5 10.5 fusion.161
  1099.1 4.0 subtract_convert_fusion.7
  1117.8 4.0 convolution_bitcast_fusion.6
  1131.0 3.3 select_add_fusion.6
  1134.2 68.6 %all-reduce.16.cloned.1.call-done = f32[1024,768]{1,0:T(8,128)} async-done(((f32[1024,768]{1,0:T(8,128)}), f32[1024,768]{1,0:T(8,128)}) %all-reduce.16.cloned.1.call-update) | async-done | bytes 3145744 | tf_op jit(solution)/shard_map/while/body/eval_jaxpr/psum | solution.py:209
  1202.9 3.4 fusion.164
  1211.4 8.1 copy.37
  1225.5 42.1 %all-reduce.1 = (f32[3,768]{1,0:T(4,128)S(1)}, f32[3072]{0:T(1024)S(1)}, f32[2,768]{1,0:T(2,128)}, f32[4,768]{1,0:T(4,128)}) all-reduce(f32[3,768]{1,0:T(4,128)S(1)} %dynamic_update_slice.19, f32[3072]{0:T(1024)S(1)} %dynamic_update_slice.20, ...), channel_id=1, replica_groups=mesh['shard'=4,'ctx'=2,'tp'=4] {'shard','ctx','tp'}, use_global_device_ids=true, to_apply=%region_29.30 | all-reduce | flops 9984 | bytes 79872 | tf_op jit(solution)/shard_map/psum | solution.py:256
  1270.2 56.7 %all-reduce.8.cloned.1.call-done = f32[768,2,768]{2,1,0:T(2,128)} async-done(((f32[768,2,768]{2,1,0:T(2,128)}), f32[768,2,768]{2,1,0:T(2,128)}) %all-reduce.8.cloned.1.call-update) | async-done | bytes 4718608
  1328.8 32.5 %reduce-scatter.6.cloned.1.call-done = f32[96,192]{1,0:T(8,128)} async-done(((f32[768,192]{1,0:T(8,128)}), f32[96,192]{1,0:T(8,128)}) %reduce-scatter.6.cloned.1.call-update) | async-done | bytes 73744 | tf_op jit(solution)/shard_map/reduce_scatter | solution.py:245
  1361.3 37.6 %reduce-scatter.4.cloned.1.call-done = f32[96,3,192]{2,0,1:T(8,128)} async-done(((f32[768,3,192]{2,0,1:T(8,128)}), f32[96,3,192]{2,0,1:T(8,128)}) %reduce-scatter.4.cloned.1.call-update) | async-done | bytes 221200 | tf_op jit(solution)/shard_map/reduce_scatter | solution.py:244
  (503 shorter events, 226.9 us)
Async XLA Ops:
  10.9 28.8 %copy-start.33 = (bf16[96,3,192]{2,1,0:T(4,128)(2,1)}, bf16[96,3,192]{2,1,0:T(4,128)(2,1)S(1)}, u32[]{:S(2)}) copy-start(bf16[96,3,192]{2,1,0:T(4,128)(2,1)S(1)} %get-tuple-element.828) | copy-start | bytes 331780 | tf_op jit(solution)/shard_map/while
  10.9 26.5 %copy-start.9 = (bf16[2,1024,768]{2,1,0:T(8,128)(2,1)S(1)}, bf16[2,1024,768]{2,1,0:T(8,128)(2,1)}, u32[]{:S(2)}) copy-start(bf16[2,1024,768]{2,1,0:T(8,128)(2,1)} %get-tuple-element.827) | copy-start | bytes 9437188 | tf_op jit(solution)/shard_map/while
  10.9 71.7 %all-gather.7.cloned.1.call-start = ((), (), s32[]{:S(2)}) async-start(), calls=%async_computation.6 | async-start | bytes 2359296 | tf_op jit(solution)/shard_map/while/body/eval_jaxpr/all_gather | solution.py:114
  52.4 9.5 copy-start.62
  57.9 149.1 %all-reduce.10.cloned.1.call-start = ((), (), s32[]{:S(2)}) async-start(), calls=%async_computation.7 | async-start | bytes 6291456 | tf_op jit(solution)/shard_map/while/body/eval_jaxpr/psum | solution.py:131
  84.2 11.4 copy-start.16
  84.2 21.9 %copy-start.20 = (bf16[1,2048,192]{1,2,0:T(8,128)(2,1)}, bf16[1,2048,192]{1,2,0:T(8,128)(2,1)S(1)}, u32[]{:S(2)}) copy-start(bf16[1,2048,192]{1,2,0:T(8,128)(2,1)S(1)} %get-tuple-element.725) | copy-start | bytes 2359300 | tf_op jit(solution)/shard_map/while
  95.6 10.5 copy-start.38
  106.1 10.7 copy-start.39
  106.1 11.4 copy-start.18
  119.9 92.2 %all-gather.9.cloned.1.call-start = ((), (), s32[]{:S(2)}) async-start(), calls=%async_computation.8 | async-start | bytes 2654208 | tf_op jit(solution)/shard_map/while/body/eval_jaxpr/all_gather | solution.py:48
  120.5 194.6 %all-reduce.12.cloned.1.call-start = ((), (), s32[]{:S(2)}) async-start(), calls=%async_computation.9 | async-start | bytes 6291456 | tf_op jit(solution)/shard_map/while/body/eval_jaxpr/psum | solution.py:142
  120.8 194.3 %copy-start.35 = (f32[768]{0:T(1024)}, f32[768]{0:T(1024)S(1)}, u32[]{:S(2)}) copy-start(f32[768]{0:T(1024)S(1)} %get-tuple-element.733) | copy-start | bytes 9220 | tf_op jit(solution)/shard_map/while
  122.3 192.8 %copy-start.45 = (f32[768]{0:T(1024)}, f32[768]{0:T(1024)S(1)}, u32[]{:S(2)}) copy-start(f32[768]{0:T(1024)S(1)} %get-tuple-element.737) | copy-start | bytes 9220 | tf_op jit(solution)/shard_map/while
  212.1 12.4 copy-start.65
  227.7 87.4 %copy-start.48 = (f32[768]{0:T(1024)S(1)}, f32[768]{0:T(1024)}, u32[]{:S(2)}) copy-start(f32[768]{0:T(1024)} %get-tuple-element.736) | copy-start | bytes 9220 | tf_op jit(solution)/shard_map/while
  227.7 194.3 %all-reduce.14.cloned.1.call-start = ((), (), s32[]{:S(2)}) async-start(), calls=%async_computation.10 | async-start | bytes 6291456 | tf_op jit(solution)/shard_map/while/body/eval_jaxpr/psum | solution.py:157
  334.7 163.7 %reduce-scatter.8.cloned.1.call-start = ((), (), s32[]{:S(2)}) async-start(), calls=%async_computation.11 | async-start | bytes 4718592 | tf_op jit(solution)/shard_map/while/body/eval_jaxpr/reduce_scatter | solution.py:187
  481.7 124.7 %all-reduce.16.cloned.1.call-start = ((), (), s32[]{:S(2)}) async-start(), calls=%async_computation.12 | async-start | bytes 6291456 | tf_op jit(solution)/shard_map/while/body/eval_jaxpr/psum | solution.py:209
  495.8 7.1 copy-start.27
  495.8 7.1 copy-start.32
  534.5 71.9 %copy-start.3 = (f32[1024,768]{1,0:T(8,128)S(1)}, f32[1024,768]{1,0:T(8,128)}, u32[]{:S(2)}) copy-start(f32[1024,768]{1,0:T(8,128)} %copy-done.1) | copy-start | bytes 9437188 | tf_op jit(solution)/shard_map/while
  610.0 27.2 %copy-start.33 = (bf16[96,3,192]{2,1,0:T(4,128)(2,1)}, bf16[96,3,192]{2,1,0:T(4,128)(2,1)S(1)}, u32[]{:S(2)}) copy-start(bf16[96,3,192]{2,1,0:T(4,128)(2,1)S(1)} %get-tuple-element.828) | copy-start | bytes 331780 | tf_op jit(solution)/shard_map/while
  610.0 24.9 %copy-start.9 = (bf16[2,1024,768]{2,1,0:T(8,128)(2,1)S(1)}, bf16[2,1024,768]{2,1,0:T(8,128)(2,1)}, u32[]{:S(2)}) copy-start(bf16[2,1024,768]{2,1,0:T(8,128)(2,1)} %get-tuple-element.827) | copy-start | bytes 9437188 | tf_op jit(solution)/shard_map/while
  610.0 69.7 %all-gather.7.cloned.1.call-start = ((), (), s32[]{:S(2)}) async-start(), calls=%async_computation.6 | async-start | bytes 2359296 | tf_op jit(solution)/shard_map/while/body/eval_jaxpr/all_gather | solution.py:114
  649.9 9.5 copy-start.62
  655.4 147.8 %all-reduce.10.cloned.1.call-start = ((), (), s32[]{:S(2)}) async-start(), calls=%async_computation.7 | async-start | bytes 6291456 | tf_op jit(solution)/shard_map/while/body/eval_jaxpr/psum | solution.py:131
  681.4 11.4 copy-start.16
  681.4 21.9 %copy-start.20 = (bf16[1,2048,192]{1,2,0:T(8,128)(2,1)}, bf16[1,2048,192]{1,2,0:T(8,128)(2,1)S(1)}, u32[]{:S(2)}) copy-start(bf16[1,2048,192]{1,2,0:T(8,128)(2,1)S(1)} %get-tuple-element.725) | copy-start | bytes 2359300 | tf_op jit(solution)/shard_map/while
  692.8 10.5 copy-start.38
  703.2 10.7 copy-start.39
  703.3 11.4 copy-start.18
  717.1 91.2 %all-gather.9.cloned.1.call-start = ((), (), s32[]{:S(2)}) async-start(), calls=%async_computation.8 | async-start | bytes 2654208 | tf_op jit(solution)/shard_map/while/body/eval_jaxpr/all_gather | solution.py:48
  717.7 193.6 %all-reduce.12.cloned.1.call-start = ((), (), s32[]{:S(2)}) async-start(), calls=%async_computation.9 | async-start | bytes 6291456 | tf_op jit(solution)/shard_map/while/body/eval_jaxpr/psum | solution.py:142
  718.2 193.0 %copy-start.35 = (f32[768]{0:T(1024)}, f32[768]{0:T(1024)S(1)}, u32[]{:S(2)}) copy-start(f32[768]{0:T(1024)S(1)} %get-tuple-element.733) | copy-start | bytes 9220 | tf_op jit(solution)/shard_map/while
  719.7 191.5 %copy-start.45 = (f32[768]{0:T(1024)}, f32[768]{0:T(1024)S(1)}, u32[]{:S(2)}) copy-start(f32[768]{0:T(1024)S(1)} %get-tuple-element.737) | copy-start | bytes 9220 | tf_op jit(solution)/shard_map/while
  808.3 12.4 copy-start.65
  823.9 87.4 %copy-start.48 = (f32[768]{0:T(1024)S(1)}, f32[768]{0:T(1024)}, u32[]{:S(2)}) copy-start(f32[768]{0:T(1024)} %get-tuple-element.736) | copy-start | bytes 9220 | tf_op jit(solution)/shard_map/while
  823.9 194.3 %all-reduce.14.cloned.1.call-start = ((), (), s32[]{:S(2)}) async-start(), calls=%async_computation.10 | async-start | bytes 6291456 | tf_op jit(solution)/shard_map/while/body/eval_jaxpr/psum | solution.py:157
  930.8 163.7 %reduce-scatter.8.cloned.1.call-start = ((), (), s32[]{:S(2)}) async-start(), calls=%async_computation.11 | async-start | bytes 4718592 | tf_op jit(solution)/shard_map/while/body/eval_jaxpr/reduce_scatter | solution.py:187
  1077.9 125.0 %all-reduce.16.cloned.1.call-start = ((), (), s32[]{:S(2)}) async-start(), calls=%async_computation.12 | async-start | bytes 6291456 | tf_op jit(solution)/shard_map/while/body/eval_jaxpr/psum | solution.py:209
  1092.0 7.1 copy-start.27
  1092.0 7.1 copy-start.32
  1131.0 71.9 %copy-start.3 = (f32[1024,768]{1,0:T(8,128)S(1)}, f32[1024,768]{1,0:T(8,128)}, u32[]{:S(2)}) copy-start(f32[1024,768]{1,0:T(8,128)} %copy-done.1) | copy-start | bytes 9437188 | tf_op jit(solution)/shard_map/while
  1211.3 115.6 %all-reduce.8.cloned.1.call-start = ((), (), s32[]{:S(2)}) async-start(), calls=%async_computation.5 | async-start | bytes 9437184
  1219.5 141.8 %reduce-scatter.6.cloned.1.call-start = ((), (), s32[]{:S(2)}) async-start(), calls=%async_computation.4 | async-start | bytes 884736 | tf_op jit(solution)/shard_map/reduce_scatter | solution.py:245
  1221.8 177.1 %reduce-scatter.4.cloned.1.call-start = ((), (), s32[]{:S(2)}) async-start(), calls=%async_computation.3 | async-start | bytes 2654208 | tf_op jit(solution)/shard_map/reduce_scatter | solution.py:244
  1221.9 46.4 %copy-start.68 = (u32[32]{0:T(128)S(1)}, u32[32]{0:T(128)}, u32[]{:S(2)}) copy-start(u32[32]{0:T(128)} %constant.281) | copy-start | bytes 388
  (115 other events, 318.0 us)
Sparse Core Ops, SparseCore 0:
  58.0 9.4 all-gather.6
  120.0 86.9 all-reduce.9
  227.8 87.2 all-reduce.11
  334.8 87.1 all-reduce.13
  481.9 10.8 reduce-scatter.7
  519.3 87.1 all-reduce.15
  655.5 8.5 all-gather.6
  717.2 85.9 all-reduce.9
  824.0 87.2 all-reduce.11
  931.0 87.2 all-reduce.13
  1078.1 10.8 reduce-scatter.7
  1115.7 87.1 all-reduce.15
Sparse Core Ops, SparseCore 1:
  122.6 31.1 all-gather.8
  719.7 30.1 all-gather.8
  1219.6 107.2 all-reduce.7
  1329.8 31.5 reduce-scatter.5
  1364.3 34.5 reduce-scatter.3
where the time goes:
time: 1410 us
  waiting for transfers between devices  782 us (55%)
  matrix products  197 us (14%)
  other arithmetic  160 us (11%)
  blocking collectives  123 us (9%)
  local copies, waits for them, and re-layouts  119 us (8%)
  between operations  16.7 us (1%)
    psum x2, waiting for transfers between devices, micro_step(): returned = lax.psum(contract_last(activated_b, ffn_full[:, 1, :]), 'tp')  174 us
    psum x2, waiting for transfers between devices, micro_step(): grad_normed = grad_second + lax.psum(ffn_part, 'tp')  172 us
    psum x2, waiting for transfers between devices, micro_step(): attended = lax.psum(contract_last(context, out_full), 'tp')  168 us
    psum x2, waiting for transfers between devices, micro_step(): lax.psum(grad_branch, 'tp')  139 us
    unnamed x4, waiting for transfers between devices  56.7 us
    all_gather x2, blocking collectives, attention_weights(): lax.all_gather(qkv_weight, ('shard', 'ctx'), axis=0, tiled=True)  44.4 us
    while x280, local copies, waits for them, and re-layouts  43.6 us
    psum x1, blocking collectives, body(): lax.psum((placed_qkv, placed_ffn, totals[5], totals[6]), ('shard', 'ctx',...  42.1 us
  transfers between devices with their start and end apart: 17, of which 11 were waited for; matrix products, arithmetic and copies ran while one was open for 7% of the time, Pallas kernels for 0%

commit v1 on v0

--- a/solution.py
+++ b/solution.py
@@ -6,6 +6,12 @@
 
 HEAD = 64
 EPSILON = 1e-12
+
+
+def gather_and_add(block, axis):
+    blocks = lax.all_gather(block, axis, axis=0, tiled=False)
+    acc = blocks.sum(axis=0)
+    return acc
 
 
 def rotate_pairs(values, offsets, direction):
@@ -206,7 +212,7 @@
         grad_branch = jnp.einsum(
             "kse,dke->sd", grad_proj, qkv_back, preferred_element_type=jnp.float32
         )
-        grad_inputs = (grad_first + lax.psum(grad_branch, "tp")).astype(jnp.bfloat16)
+        grad_inputs = (grad_first + gather_and_add(grad_branch, "tp")).astype(jnp.bfloat16)
         grad_shift = jnp.stack(
             [
                 jnp.sum(normed_part, axis=0),

time: 1410 us -> 1490 us (1.057)
  waiting for transfers between devices: 782 us -> 854 us
    all_gather x0 -> x2, waiting for transfers between devices: none -> 211 us  [gather_and_add(): blocks = lax.all_gather(block, axis, axis=0, tiled=False)]
    psum x2 -> x0, waiting for transfers between devices: 139 us -> none  [micro_step(): lax.psum(grad_branch, 'tp')]
    reduce_sum x0 -> x2, other arithmetic: none -> 15.2 us  [gather_and_add(): acc = blocks.sum(axis=0)]
  transfers between devices with their start and end apart: 17 -> 17, of which waited for: 11 -> 11; matrix products, arithmetic and copies ran while one was open for 7% -> 6% of each run, Pallas kernels for 0% -> 0%
where the time goes in v1:
time: 1490 us; the launch traced here: 1480 us
  waiting for transfers between devices  854 us (57%)
  matrix products  190 us (13%)
  other arithmetic  174 us (12%)
  blocking collectives  122 us (8%)
  local copies, waits for them, and re-layouts  117 us (8%)
  between operations  16.7 us (1%)
    all_gather x2, waiting for transfers between devices, gather_and_add(): blocks = lax.all_gather(block, axis, axis=0, tiled=False)  211 us
    psum x2, waiting for transfers between devices, micro_step(): returned = lax.psum(contract_last(activated_b, ffn_full[:, 1, :]), 'tp')  174 us
    psum x2, waiting for transfers between devices, micro_step(): grad_normed = grad_second + lax.psum(ffn_part, 'tp')  173 us
    psum x2, waiting for transfers between devices, micro_step(): attended = lax.psum(contract_last(context, out_full), 'tp')  168 us
    unnamed x4, waiting for transfers between devices  56.7 us
    all_gather x2, blocking collectives, attention_weights(): lax.all_gather(qkv_weight, ('shard', 'ctx'), axis=0, tiled=True)  44.4 us
    psum x1, blocking collectives, body(): lax.psum((placed_qkv, placed_ffn, totals[5], totals[6]), ('shard', 'ctx',...  42.1 us
    while x280, local copies, waits for them, and re-layouts  41.7 us
  transfers between devices with their start and end apart: 17, of which 11 were waited for; matrix products, arithmetic and copies ran while one was open for 6% of the time, Pallas kernels for 0%

profile of v1, /device:TPU:0, one launch (start us, length us, event | category | flops | bytes accessed | tf_op | source)
XLA Modules:
  0.0 1484.4 jit_solution(11991651762972356146)
XLA Ops:
  10.9 1278.2 %while.29 = (s32[]{:T(128)}, f32[768,3,192]{0,2,1:T(8,128)}, f32[768,192]{0,1:T(8,128)}, f32[768,2,768]{2,0,1:T(8,128)}, f32[3,192]{1,0:T(4,128)}, /*index=5*/f3...) while((s32[]{:T(128)}, f32[768,3,192]{0,2,1:T(8,128)}, ...), condition=%wide.region_25.26_spmd.clone, body=%wide.region_0.25_spmd.clone.sunk | while | flops 15949049856 | bytes 1011955520 | solution.py:246
  10.9 23.1 %all_gather.54 = bf16[768,3,192]{2,1,0:T(4,128)(2,1)} all-gather(bf16[96,3,192]{2,1,0:T(4,128)(2,1)S(1)} %get-tuple-element.830), channel_id=1, replica_groups=mesh['shard'=4,'ctx'=2,'tp'=4] {'shard','ctx'}, dimensions={0}, use_global_device_ids=true | all-gather | bytes 995328 | tf_op jit(solution)/shard_map/while/body/eval_jaxpr/all_gather | solution.py:48
  34.0 3.4 copy.39
  48.1 4.2 subtract_convert_fusion.6
  63.8 16.3 %all_gather.53 = bf16[768,192]{1,0:T(8,128)(2,1)} all-gather(bf16[96,192]{1,0:T(8,128)(2,1)} %get-tuple-element.834), channel_id=1, replica_groups=mesh['shard'=4,'ctx'=2,'tp'=4] {'shard','ctx'}, dimensions={0}, use_global_device_ids=true | all-gather | bytes 331776 | tf_op jit(solution)/shard_map/while/body/eval_jaxpr/all_gather | solution.py:49
  84.7 11.0 fusion.150
  95.6 10.4 fusion.151
  106.1 10.6 fusion.152
  122.3 84.8 %all-reduce.9.cloned.1.call-done = f32[1024,768]{1,0:T(8,128)} async-done(((f32[1024,768]{1,0:T(8,128)}), f32[1024,768]{1,0:T(8,128)}) %all-reduce.9.cloned.1.call-update) | async-done | bytes 3145744 | tf_op jit(solution)/shard_map/while/body/eval_jaxpr/psum | solution.py:137
  212.1 11.2 multiply_convert_fusion.4
  227.9 87.1 %all-reduce.11.cloned.1.call-done = f32[1024,768]{1,0:T(8,128)} async-done(((f32[1024,768]{1,0:T(8,128)}), f32[1024,768]{1,0:T(8,128)}) %all-reduce.11.cloned.1.call-update) | async-done | bytes 3145744 | tf_op jit(solution)/shard_map/while/body/eval_jaxpr/psum | solution.py:148
  331.4 3.1 fusion.159
  335.6 86.3 %all-reduce.13.cloned.1.call-done = f32[1024,768]{1,0:T(8,128)} async-done(((f32[1024,768]{1,0:T(8,128)}), f32[1024,768]{1,0:T(8,128)}) %all-reduce.13.cloned.1.call-update) | async-done | bytes 3145744 | tf_op jit(solution)/shard_map/while/body/eval_jaxpr/psum | solution.py:163
  421.9 3.6 multiply_reduce_fusion.13
  430.2 11.4 fusion.160
  441.6 16.4 %multiply_reduce_fusion.14 = (f32[3,1024]{1,0:T(4,128)}, f32[3,1024,2048]{2,1,0:T(8,128)}) fusion(f32[3,1024,2048]{2,1,0:T(8,128)} %get-tuple-element.731, f32[3,1024]{1,0:T(4,128)S(1)} %log_add_fusion.2, bf16[1024,3,64]{0,2,1:T(8,128)(2,1)} %bitcast.227, bf16[2048,3,64]{0,2,1:T(8,128)(2,1)} %bitcast.231), kind=kOutput, calls=%fused_computation.1.clone.1 | convolution fusion | flops 824177664 | bytes 51535872 | tf_op jit(solution)/shard_map/while/body/eval_jaxpr/shd,thd->hst/dot_general | solution.py:177
  458.0 16.8 %multiply_convert_fusion.5 = bf16[3,1024,2048]{2,1,0:T(8,128)(2,1)S(1)} fusion(f32[3,1024,2048]{2,1,0:T(8,128)} %get-tuple-element.750, f32[3,1024,2048]{2,1,0:T(8,128)} %get-tuple-element.731, f32[3,1024]{1,0:T(4,128)} %get-tuple-element.751, f32[3,1024]{1,0:T(4,128)S(1)} %log_add_fusion.2), kind=kLoop, calls=%fused_computation.clone.1 | loop fusion | flops 25165824 | bytes 62939136 | tf_op jit(solution)/shard_map/while/body/eval_jaxpr/convert_element_type | solution.py:181
  482.1 9.7 fusion.161
  498.9 3.8 subtract_convert_fusion.7
  531.7 106.1 %all-gather.16.cloned.1.call-done = f32[4096,768]{1,0:T(8,128)} async-done(((f32[1024,768]{1,0:T(8,128)}), f32[4096,768]{1,0:T(8,128)}) %all-gather.16.cloned.1.call-update) | async-done | bytes 12582928 | tf_op jit(solution)/shard_map/while/body/eval_jaxpr/all_gather | solution.py:12
  637.8 7.6 reduce_sum.294
  645.4 3.4 fusion.164
  649.1 21.4 %all_gather.54 = bf16[768,3,192]{2,1,0:T(4,128)(2,1)} all-gather(bf16[96,3,192]{2,1,0:T(4,128)(2,1)S(1)} %get-tuple-element.830), channel_id=1, replica_groups=mesh['shard'=4,'ctx'=2,'tp'=4] {'shard','ctx'}, dimensions={0}, use_global_device_ids=true | all-gather | bytes 995328 | tf_op jit(solution)/shard_map/while/body/eval_jaxpr/all_gather | solution.py:48
  670.4 3.4 copy.39
  684.6 4.2 subtract_convert_fusion.6
  700.2 16.0 %all_gather.53 = bf16[768,192]{1,0:T(8,128)(2,1)} all-gather(bf16[96,192]{1,0:T(8,128)(2,1)} %get-tuple-element.834), channel_id=1, replica_groups=mesh['shard'=4,'ctx'=2,'tp'=4] {'shard','ctx'}, dimensions={0}, use_global_device_ids=true | all-gather | bytes 331776 | tf_op jit(solution)/shard_map/while/body/eval_jaxpr/all_gather | solution.py:49
  720.8 11.0 fusion.150
  731.7 10.4 fusion.151
  742.2 10.6 fusion.152
  758.7 83.5 %all-reduce.9.cloned.1.call-done = f32[1024,768]{1,0:T(8,128)} async-done(((f32[1024,768]{1,0:T(8,128)}), f32[1024,768]{1,0:T(8,128)}) %all-reduce.9.cloned.1.call-update) | async-done | bytes 3145744 | tf_op jit(solution)/shard_map/while/body/eval_jaxpr/psum | solution.py:137
  847.2 11.2 multiply_convert_fusion.4
  863.0 87.2 %all-reduce.11.cloned.1.call-done = f32[1024,768]{1,0:T(8,128)} async-done(((f32[1024,768]{1,0:T(8,128)}), f32[1024,768]{1,0:T(8,128)}) %all-reduce.11.cloned.1.call-update) | async-done | bytes 3145744 | tf_op jit(solution)/shard_map/while/body/eval_jaxpr/psum | solution.py:148
  966.5 3.1 fusion.159
  970.7 86.3 %all-reduce.13.cloned.1.call-done = f32[1024,768]{1,0:T(8,128)} async-done(((f32[1024,768]{1,0:T(8,128)}), f32[1024,768]{1,0:T(8,128)}) %all-reduce.13.cloned.1.call-update) | async-done | bytes 3145744 | tf_op jit(solution)/shard_map/while/body/eval_jaxpr/psum | solution.py:163
  1057.0 3.6 multiply_reduce_fusion.13
  1065.3 11.4 fusion.160
  1076.8 16.4 %multiply_reduce_fusion.14 = (f32[3,1024]{1,0:T(4,128)}, f32[3,1024,2048]{2,1,0:T(8,128)}) fusion(f32[3,1024,2048]{2,1,0:T(8,128)} %get-tuple-element.731, f32[3,1024]{1,0:T(4,128)S(1)} %log_add_fusion.2, bf16[1024,3,64]{0,2,1:T(8,128)(2,1)} %bitcast.227, bf16[2048,3,64]{0,2,1:T(8,128)(2,1)} %bitcast.231), kind=kOutput, calls=%fused_computation.1.clone.1 | convolution fusion | flops 824177664 | bytes 51535872 | tf_op jit(solution)/shard_map/while/body/eval_jaxpr/shd,thd->hst/dot_general | solution.py:177
  1093.1 16.8 %multiply_convert_fusion.5 = bf16[3,1024,2048]{2,1,0:T(8,128)(2,1)S(1)} fusion(f32[3,1024,2048]{2,1,0:T(8,128)} %get-tuple-element.750, f32[3,1024,2048]{2,1,0:T(8,128)} %get-tuple-element.731, f32[3,1024]{1,0:T(4,128)} %get-tuple-element.751, f32[3,1024]{1,0:T(4,128)S(1)} %log_add_fusion.2), kind=kLoop, calls=%fused_computation.clone.1 | loop fusion | flops 25165824 | bytes 62939136 | tf_op jit(solution)/shard_map/while/body/eval_jaxpr/convert_element_type | solution.py:181
  1117.0 9.7 fusion.161
  1133.9 4.1 subtract_convert_fusion.7
  1168.4 104.6 %all-gather.16.cloned.1.call-done = f32[4096,768]{1,0:T(8,128)} async-done(((f32[1024,768]{1,0:T(8,128)}), f32[4096,768]{1,0:T(8,128)}) %all-gather.16.cloned.1.call-update) | async-done | bytes 12582928 | tf_op jit(solution)/shard_map/while/body/eval_jaxpr/all_gather | solution.py:12
  1273.0 7.6 reduce_sum.294
  1280.6 3.4 fusion.164
  1289.1 8.1 copy.37
  1303.2 42.1 %all-reduce.1 = (f32[3,768]{1,0:T(4,128)S(1)}, f32[3072]{0:T(1024)S(1)}, f32[2,768]{1,0:T(2,128)}, f32[4,768]{1,0:T(4,128)}) all-reduce(f32[3,768]{1,0:T(4,128)S(1)} %dynamic_update_slice.19, f32[3072]{0:T(1024)S(1)} %dynamic_update_slice.20, ...), channel_id=1, replica_groups=mesh['shard'=4,'ctx'=2,'tp'=4] {'shard','ctx','tp'}, use_global_device_ids=true, to_apply=%region_29.30 | all-reduce | flops 9984 | bytes 79872 | tf_op jit(solution)/shard_map/psum | solution.py:262
  1347.9 56.7 %all-reduce.7.cloned.1.call-done = f32[768,2,768]{2,1,0:T(2,128)} async-done(((f32[768,2,768]{2,1,0:T(2,128)}), f32[768,2,768]{2,1,0:T(2,128)}) %all-reduce.7.cloned.1.call-update) | async-done | bytes 4718608
  1406.5 32.5 %reduce-scatter.6.cloned.1.call-done = f32[96,192]{1,0:T(8,128)} async-done(((f32[768,192]{1,0:T(8,128)}), f32[96,192]{1,0:T(8,128)}) %reduce-scatter.6.cloned.1.call-update) | async-done | bytes 73744 | tf_op jit(solution)/shard_map/reduce_scatter | solution.py:251
  1439.0 37.6 %reduce-scatter.4.cloned.1.call-done = f32[96,3,192]{2,0,1:T(8,128)} async-done(((f32[768,3,192]{2,0,1:T(8,128)}), f32[96,3,192]{2,0,1:T(8,128)}) %reduce-scatter.4.cloned.1.call-update) | async-done | bytes 221200 | tf_op jit(solution)/shard_map/reduce_scatter | solution.py:250
  (505 shorter events, 227.2 us)
Async XLA Ops:
  10.9 28.8 %copy-start.32 = (bf16[96,3,192]{2,1,0:T(4,128)(2,1)}, bf16[96,3,192]{2,1,0:T(4,128)(2,1)S(1)}, u32[]{:S(2)}) copy-start(bf16[96,3,192]{2,1,0:T(4,128)(2,1)S(1)} %get-tuple-element.830) | copy-start | bytes 331780 | tf_op jit(solution)/shard_map/while
  10.9 26.5 %copy-start.10 = (bf16[2,1024,768]{2,1,0:T(8,128)(2,1)S(1)}, bf16[2,1024,768]{2,1,0:T(8,128)(2,1)}, u32[]{:S(2)}) copy-start(bf16[2,1024,768]{2,1,0:T(8,128)(2,1)} %get-tuple-element.829) | copy-start | bytes 9437188 | tf_op jit(solution)/shard_map/while
  10.9 71.7 %all-gather.12.cloned.1.call-start = ((), (), s32[]{:S(2)}) async-start(), calls=%async_computation.6 | async-start | bytes 2359296 | tf_op jit(solution)/shard_map/while/body/eval_jaxpr/all_gather | solution.py:120
  52.4 9.5 copy-start.61
  57.9 149.1 %all-reduce.9.cloned.1.call-start = ((), (), s32[]{:S(2)}) async-start(), calls=%async_computation.7 | async-start | bytes 6291456 | tf_op jit(solution)/shard_map/while/body/eval_jaxpr/psum | solution.py:137
  84.2 11.4 copy-start.16
  84.2 21.9 %copy-start.19 = (bf16[1,2048,192]{1,2,0:T(8,128)(2,1)}, bf16[1,2048,192]{1,2,0:T(8,128)(2,1)S(1)}, u32[]{:S(2)}) copy-start(bf16[1,2048,192]{1,2,0:T(8,128)(2,1)S(1)} %get-tuple-element.725) | copy-start | bytes 2359300 | tf_op jit(solution)/shard_map/while
  95.6 10.5 copy-start.37
  106.1 10.7 copy-start.38
  106.1 11.4 copy-start.17
  119.9 92.2 %all-gather.14.cloned.1.call-start = ((), (), s32[]{:S(2)}) async-start(), calls=%async_computation.8 | async-start | bytes 2654208 | tf_op jit(solution)/shard_map/while/body/eval_jaxpr/all_gather | solution.py:54
  120.5 194.5 %all-reduce.11.cloned.1.call-start = ((), (), s32[]{:S(2)}) async-start(), calls=%async_computation.9 | async-start | bytes 6291456 | tf_op jit(solution)/shard_map/while/body/eval_jaxpr/psum | solution.py:148
  120.8 194.2 %copy-start.34 = (f32[768]{0:T(1024)}, f32[768]{0:T(1024)S(1)}, u32[]{:S(2)}) copy-start(f32[768]{0:T(1024)S(1)} %get-tuple-element.733) | copy-start | bytes 9220 | tf_op jit(solution)/shard_map/while
  122.3 192.7 %copy-start.44 = (f32[768]{0:T(1024)}, f32[768]{0:T(1024)S(1)}, u32[]{:S(2)}) copy-start(f32[768]{0:T(1024)S(1)} %get-tuple-element.737) | copy-start | bytes 9220 | tf_op jit(solution)/shard_map/while
  212.1 12.4 copy-start.64
  227.6 87.4 %copy-start.47 = (f32[768]{0:T(1024)S(1)}, f32[768]{0:T(1024)}, u32[]{:S(2)}) copy-start(f32[768]{0:T(1024)} %get-tuple-element.736) | copy-start | bytes 9220 | tf_op jit(solution)/shard_map/while
  227.6 194.3 %all-reduce.13.cloned.1.call-start = ((), (), s32[]{:S(2)}) async-start(), calls=%async_computation.10 | async-start | bytes 6291456 | tf_op jit(solution)/shard_map/while/body/eval_jaxpr/psum | solution.py:163
  334.6 159.8 %reduce-scatter.8.cloned.1.call-start = ((), (), s32[]{:S(2)}) async-start(), calls=%async_computation.11 | async-start | bytes 4718592 | tf_op jit(solution)/shard_map/while/body/eval_jaxpr/reduce_scatter | solution.py:193
  481.6 156.3 %all-gather.16.cloned.1.call-start = ((), (), s32[]{:S(2)}) async-start(), calls=%async_computation.12 | async-start | bytes 15728640 | tf_op jit(solution)/shard_map/while/body/eval_jaxpr/all_gather | solution.py:12
  491.7 7.2 copy-start.26
  491.7 7.2 copy-start.31
  637.8 7.6 copy-start.3
  649.0 27.2 %copy-start.32 = (bf16[96,3,192]{2,1,0:T(4,128)(2,1)}, bf16[96,3,192]{2,1,0:T(4,128)(2,1)S(1)}, u32[]{:S(2)}) copy-start(bf16[96,3,192]{2,1,0:T(4,128)(2,1)S(1)} %get-tuple-element.830) | copy-start | bytes 331780 | tf_op jit(solution)/shard_map/while
  649.0 24.9 %copy-start.10 = (bf16[2,1024,768]{2,1,0:T(8,128)(2,1)S(1)}, bf16[2,1024,768]{2,1,0:T(8,128)(2,1)}, u32[]{:S(2)}) copy-start(bf16[2,1024,768]{2,1,0:T(8,128)(2,1)} %get-tuple-element.829) | copy-start | bytes 9437188 | tf_op jit(solution)/shard_map/while
  649.0 69.7 %all-gather.12.cloned.1.call-start = ((), (), s32[]{:S(2)}) async-start(), calls=%async_computation.6 | async-start | bytes 2359296 | tf_op jit(solution)/shard_map/while/body/eval_jaxpr/all_gather | solution.py:120
  688.8 9.5 copy-start.61
  694.3 147.8 %all-reduce.9.cloned.1.call-start = ((), (), s32[]{:S(2)}) async-start(), calls=%async_computation.7 | async-start | bytes 6291456 | tf_op jit(solution)/shard_map/while/body/eval_jaxpr/psum | solution.py:137
  720.3 11.4 copy-start.16
  720.3 21.9 %copy-start.19 = (bf16[1,2048,192]{1,2,0:T(8,128)(2,1)}, bf16[1,2048,192]{1,2,0:T(8,128)(2,1)S(1)}, u32[]{:S(2)}) copy-start(bf16[1,2048,192]{1,2,0:T(8,128)(2,1)S(1)} %get-tuple-element.725) | copy-start | bytes 2359300 | tf_op jit(solution)/shard_map/while
  731.7 10.5 copy-start.37
  742.2 10.7 copy-start.38
  742.2 11.4 copy-start.17
  756.0 91.2 %all-gather.14.cloned.1.call-start = ((), (), s32[]{:S(2)}) async-start(), calls=%async_computation.8 | async-start | bytes 2654208 | tf_op jit(solution)/shard_map/while/body/eval_jaxpr/all_gather | solution.py:54
  756.6 193.5 %all-reduce.11.cloned.1.call-start = ((), (), s32[]{:S(2)}) async-start(), calls=%async_computation.9 | async-start | bytes 6291456 | tf_op jit(solution)/shard_map/while/body/eval_jaxpr/psum | solution.py:148
  757.2 192.9 %copy-start.34 = (f32[768]{0:T(1024)}, f32[768]{0:T(1024)S(1)}, u32[]{:S(2)}) copy-start(f32[768]{0:T(1024)S(1)} %get-tuple-element.733) | copy-start | bytes 9220 | tf_op jit(solution)/shard_map/while
  758.7 191.5 %copy-start.44 = (f32[768]{0:T(1024)}, f32[768]{0:T(1024)S(1)}, u32[]{:S(2)}) copy-start(f32[768]{0:T(1024)S(1)} %get-tuple-element.737) | copy-start | bytes 9220 | tf_op jit(solution)/shard_map/while
  847.2 12.4 copy-start.64
  862.7 87.4 %copy-start.47 = (f32[768]{0:T(1024)S(1)}, f32[768]{0:T(1024)}, u32[]{:S(2)}) copy-start(f32[768]{0:T(1024)} %get-tuple-element.736) | copy-start | bytes 9220 | tf_op jit(solution)/shard_map/while
  862.7 194.3 %all-reduce.13.cloned.1.call-start = ((), (), s32[]{:S(2)}) async-start(), calls=%async_computation.10 | async-start | bytes 6291456 | tf_op jit(solution)/shard_map/while/body/eval_jaxpr/psum | solution.py:163
  969.7 159.6 %reduce-scatter.8.cloned.1.call-start = ((), (), s32[]{:S(2)}) async-start(), calls=%async_computation.11 | async-start | bytes 4718592 | tf_op jit(solution)/shard_map/while/body/eval_jaxpr/reduce_scatter | solution.py:193
  1116.7 156.3 %all-gather.16.cloned.1.call-start = ((), (), s32[]{:S(2)}) async-start(), calls=%async_computation.12 | async-start | bytes 15728640 | tf_op jit(solution)/shard_map/while/body/eval_jaxpr/all_gather | solution.py:12
  1126.6 7.2 copy-start.26
  1126.7 7.2 copy-start.31
  1273.0 7.6 copy-start.3
  1289.0 115.6 %all-reduce.7.cloned.1.call-start = ((), (), s32[]{:S(2)}) async-start(), calls=%async_computation.5 | async-start | bytes 9437184
  1297.2 141.8 %reduce-scatter.6.cloned.1.call-start = ((), (), s32[]{:S(2)}) async-start(), calls=%async_computation.4 | async-start | bytes 884736 | tf_op jit(solution)/shard_map/reduce_scatter | solution.py:251
  1299.5 177.1 %reduce-scatter.4.cloned.1.call-start = ((), (), s32[]{:S(2)}) async-start(), calls=%async_computation.3 | async-start | bytes 2654208 | tf_op jit(solution)/shard_map/reduce_scatter | solution.py:250
  1299.6 46.4 %copy-start.67 = (u32[32]{0:T(128)S(1)}, u32[32]{0:T(128)}, u32[]{:S(2)}) copy-start(u32[32]{0:T(128)} %constant.281) | copy-start | bytes 388
  (115 other events, 306.1 us)
Sparse Core Ops, SparseCore 0:
  58.0 9.4 all-gather.11
  120.0 86.9 all-reduce.8
  227.7 87.2 all-reduce.10
  334.7 87.1 all-reduce.12
  481.7 10.8 reduce-scatter.7
  515.2 122.5 all-gather.15
  694.5 8.5 all-gather.11
  756.1 85.9 all-reduce.8
  862.9 87.2 all-reduce.10
  969.8 87.1 all-reduce.12
  1116.8 10.8 reduce-scatter.7
  1150.5 122.4 all-gather.15
Sparse Core Ops, SparseCore 1:
  122.6 31.1 all-gather.13
  758.7 30.1 all-gather.13
  1297.3 107.2 all-reduce.6
  1407.5 31.5 reduce-scatter.5
  1442.0 34.5 reduce-scatter.3
